TPU v7x, 512 devices: a whole 4x8x8 slice. The times are simulated.
512 devices in a mesh: pool: 64 (over y, z), tensor: 8 (over x, core).
Axes of the slice: x: 4, y: 8, z: 8, core: 2. Of those that a mesh axis runs over, the one named last changes fastest.
Arguments:
- tokens: bfloat16 [2, 256, 8192], P(None, None, 'tensor'), may hold values from -6 to 6
- gate_up_weight: bfloat16 [8192, 2, 28672], P('tensor', None, 'pool'), may hold values from -0.0625 to 0.0625
- down_weight: bfloat16 [28672, 8192], P('pool', 'tensor'), may hold values from -0.03125 to 0.03125
- shrink_store: bfloat16 [64, 2, 8192, 64], P('pool', None, 'tensor'), may hold values from -0.0625 to 0.0625
- expand_store: bfloat16 [64, 2, 64, 28672], P('pool', None, 'tensor'), may hold values from -0.75 to 0.75
- block_adapter: int32 [2, 2], replicated, may hold values from 0 to 63
- block_live: int32 [2, 2], replicated, may hold values from 1 to 128, 192 in all within a row
- adapter_slot: int32 [64], replicated, may hold values from 0 to 63, each once
Outputs:
- layer_out: bfloat16 [2, 256, 8192], P(None, 'pool', 'tensor')
Inputs may be any that keep to these rules, and one draw needn't show every extreme that they name: Each storage slot holds exactly one adapter; adapter a is stored on index adapter_slot[a] of pool; each index of pool holds exactly one storage slot. `block_live`: rows of a block after its live rows are padding; the live rows of one decode step sum to 192.
All inputs are finite; a program needn't handle non-finite values.
Results may differ from a plain program's by a relative error of at most 0.0049.
Values may be sent and summed in bfloat16 or wider, within the bound.
A program may use at most 64 MiB of HBM per device.

v0:
```python
import jax
import jax.numpy as jnp
from jax import lax
from jax.sharding import PartitionSpec as P

BLK = 128
NBLK = 2


def from_root(shard, axis, root):
    mine = lax.axis_index(axis) == root
    return lax.psum(jnp.where(mine, shard, jnp.zeros_like(shard)), axis)


def fetch_split(shrink_store, expand_store, slots):
    per_owner = shrink_store.shape[0]
    pool_count = lax.axis_size("pool")
    me = lax.axis_index("pool")
    shrink_pages = []
    outgoing = []
    owner_list = []
    for slot in slots:
        owner = slot // per_owner
        local = slot % per_owner
        shrink_here = lax.dynamic_index_in_dim(shrink_store, local, 0, keepdims=False)
        shrink_pages.append(from_root(shrink_here, "pool", owner))
        expand_here = lax.dynamic_index_in_dim(expand_store, local, 0, keepdims=False)
        kinds, ranks, units = expand_here.shape
        split_cols = expand_here.reshape(kinds, ranks, pool_count, units // pool_count).transpose(
            2, 0, 1, 3
        )
        mine = (owner == me).astype(split_cols.dtype)
        outgoing.append(split_cols * mine)
        owner_list.append(owner)
    received = lax.all_to_all(
        jnp.stack(outgoing, axis=1), "pool", split_axis=0, concat_axis=0, tiled=True
    )
    expand_pages = []
    for block_index in range(len(slots)):
        from_owner = lax.dynamic_index_in_dim(received, owner_list[block_index], 0, keepdims=False)
        expand_pages.append(from_owner[block_index])
    return (shrink_pages, expand_pages)


def shards(
    tokens,
    gate_up_weight,
    down_weight,
    shrink_store,
    expand_store,
    block_adapter,
    block_live,
    adapter_slot,
):
    highest = lax.Precision.HIGHEST
    width_local = gate_up_weight.shape[0]
    units = gate_up_weight.shape[2]
    total_rows = tokens.shape[1]
    flat_weight = gate_up_weight.reshape(width_local, 2 * units)
    rows_here = total_rows // lax.axis_size("pool")
    positions = lax.axis_index("pool") * rows_here + jnp.arange(rows_here)
    owners = positions // BLK
    results = []
    for decode_step in range(tokens.shape[0]):
        inputs = tokens[decode_step]
        slots = [
            adapter_slot[block_adapter[decode_step, block_index]] for block_index in range(NBLK)
        ]
        shrink_pages, expand_list = fetch_split(shrink_store, expand_store, slots)
        shrunk_list = []
        for block_index in range(NBLK):
            block_rows = inputs[block_index * BLK : (block_index + 1) * BLK]
            shrunk_list.append(
                jnp.einsum(
                    "nd,kdc->knc",
                    block_rows,
                    shrink_pages[block_index],
                    preferred_element_type=jnp.float32,
                )
            )
        shrunk = jnp.concatenate(shrunk_list, axis=1)
        rank_share = lax.psum_scatter(shrunk, "tensor", scatter_dimension=2, tiled=True)
        terms = [
            jnp.einsum(
                "knc,kcf->nkf",
                rank_share[:, block_index * BLK : (block_index + 1) * BLK],
                expand_list[block_index].astype(jnp.float32),
                precision=highest,
            )
            for block_index in range(NBLK)
        ]
        adapted = jnp.concatenate(terms, axis=0)
        partial_sums = (
            jnp.dot(inputs, flat_weight, preferred_element_type=jnp.float32).reshape(
                total_rows, 2, units
            )
            + adapted
        )
        totals = lax.psum(partial_sums, "tensor")
        hidden = (jax.nn.silu(totals[:, 0]) * totals[:, 1]).astype(jnp.bfloat16)

        def project(first_row, row_count, hidden=hidden):
            return jnp.dot(hidden, down_weight, preferred_element_type=jnp.float32)

        summed = lax.psum_scatter(
            project(jnp.int32(0), rows_here * lax.axis_size("pool")),
            "pool",
            scatter_dimension=0,
            tiled=True,
        )
        live = jnp.sum(
            (owners[:, None] == jnp.arange(NBLK)[None, :]) * block_live[decode_step][None, :],
            axis=1,
        )
        keep = (positions % BLK < live).astype(jnp.float32)
        results.append((summed * keep[:, None]).astype(jnp.bfloat16))
    return jnp.stack(results)


def solution(mesh):
    return jax.shard_map(
        shards,
        mesh=mesh,
        in_specs=(
            P(None, None, "tensor"),
            P("tensor", None, "pool"),
            P("pool", "tensor"),
            P("pool", None, "tensor", None),
            P("pool", None, "tensor", None),
            P(),
            P(),
            P(),
        ),
        out_specs=P(None, "pool", "tensor"),
        check_vma=False,
    )
```

profile of v0, /device:TPU:1, one launch (start us, length us, event | category | flops | bytes accessed | tf_op | source)
XLA Modules:
  0.0 629.8 jit_solution(3497687153931601568)
XLA Ops:
  6.5 1.5 fusion.46
  15.4 1.5 fusion.47
  19.4 3.2 broadcast_multiply_fusion.3
  22.6 2.4 mul.102
  24.9 3.4 mul.106
  28.3 2.4 copy_bitcast_fusion.2
  30.7 1.6 pad_maximum_fusion
  32.3 17.4 %all-to-all-start = ((bf16[64,2,2,8,448]{4,3,2,1,0:T(8,128)(2,1)}), bf16[64,2,2,8,448]{4,3,2,1,0:T(8,128)(2,1)}, u32[]{:S(2)}, u32[]{:S(2)}) async-start(bf16[64,2,2,8,448]{4,3,2,1,0:T(8,128)(2,1)} %pad_maximum_fusion), calls=%async_computation | async-start | bytes 4194304 | tf_op jit(solution)/shard_map/all_to_all | solution.py:35
  49.7 2.4 mul.118
  52.1 3.4 mul.122
  55.4 2.4 copy_bitcast_fusion
  57.8 1.5 pad_maximum_fusion.1
  59.3 38.6 %all-to-all-done = bf16[64,2,2,8,448]{4,3,2,1,0:T(8,128)(2,1)} async-done(((bf16[64,2,2,8,448]{4,3,2,1,0:T(8,128)(2,1)}), bf16[64,2,2,8,448]{4,3,2,1,0:T(8,128)(2,1)}, u32[]{:S(2)}, u32[]{:S(2)}) %all-to-all-start) | async-done | bytes 1835040 | tf_op jit(solution)/shard_map/all_to_all | solution.py:35
  98.0 14.5 %all-to-all-start.1 = ((bf16[64,2,2,8,448]{4,3,2,1,0:T(8,128)(2,1)}), bf16[64,2,2,8,448]{4,3,2,1,0:T(8,128)(2,1)}, u32[]{:S(2)}, u32[]{:S(2)}) async-start(bf16[64,2,2,8,448]{4,3,2,1,0:T(8,128)(2,1)} %pad_maximum_fusion.1), calls=%async_computation.2 | async-start | bytes 4194304 | tf_op jit(solution)/shard_map/all_to_all | solution.py:35
  112.5 0.0 all-reduce.13.cloned.1.call-start
  115.1 1.1 select_bitcast_fusion.3
  116.2 0.0 all-reduce.13.cloned.1.call-update
  116.2 0.0 reduce-scatter.3.cloned.1.call-start
  123.8 176.4 %all-reduce.13.cloned.1.call-done = (bf16[2,1024,64]{1,2,0:T(8,128)(2,1)}, bf16[2,1024,64]{1,2,0:T(8,128)(2,1)}, bf16[2,1024,64]{1,2,0:T(8,128)(2,1)}, bf16[2,1024,64]{1,2,0:T(8,128)(2,1)}) async-done(((bf16[2,1024,64]{1,2,0:T(8,128)(2,1)}, bf16[2,1024,64]{1,2,0:T(8,128)(2,1)}, bf16[2,1024,64]{1,2,0:T(8,128)(2,1)}, bf16[2,1024,64]{1,2,0:T(8,128)(2,1)}), (bf16[2,1024,64]{1,2,0:T(8,128)(2,1)}, ...) | async-done | bytes 1048592 | tf_op jit(solution)/shard_map/psum | solution.py:12
  300.2 1.2 convolution_bitcast_fusion.6
  301.4 1.2 convolution_bitcast_fusion.7
  302.6 0.7 pad_maximum_fusion.2
  303.2 0.0 reduce-scatter.3.cloned.1.call-update
  303.3 0.0 reduce-scatter.5.cloned.1.call-start
  303.3 1.2 convolution_bitcast_fusion.4
  304.5 0.2 convolution_bitcast_fusion.5
  304.8 0.7 pad_maximum_fusion.3
  305.4 0.0 reduce-scatter.5.cloned.1.call-update
  305.5 0.2 all-reduce.11.cloned.1.call-start
  305.7 33.0 %reduce-scatter.3.cloned.1.call-done = f32[2,256,8]{1,2,0:T(8,128)} async-done(((f32[2,256,64]{1,2,0:T(8,128)}), f32[2,256,8]{1,2,0:T(8,128)}) %reduce-scatter.3.cloned.1.call-update) | async-done | bytes 16400 | tf_op jit(solution)/shard_map/reduce_scatter | solution.py:82
  338.7 1.1 convolution_bitcast_fusion.3
  339.9 1.1 convolution_bitcast_fusion.2
  341.0 1.6 fusion.4
  342.6 33.9 %reduce-scatter.5.cloned.1.call-done = f32[2,256,8]{1,2,0:T(8,128)} async-done(((f32[2,256,64]{1,2,0:T(8,128)}), f32[2,256,8]{1,2,0:T(8,128)}) %reduce-scatter.5.cloned.1.call-update) | async-done | bytes 16400 | tf_op jit(solution)/shard_map/reduce_scatter | solution.py:82
  376.5 1.1 convolution_bitcast_fusion.1
  377.7 1.1 convolution_bitcast_fusion
  378.8 1.6 fusion.7
  380.4 0.0 all-reduce.11.cloned.1.call-update
  380.5 0.0 all-reduce.9.cloned.1.call-start
  380.5 74.4 %all-reduce.11.cloned.1.call-done = (f32[256,2,448]{0,2,1:T(8,128)}, f32[256,2,448]{0,2,1:T(8,128)}) async-done(((f32[256,2,448]{0,2,1:T(8,128)}, f32[256,2,448]{0,2,1:T(8,128)}), (f32[256,2,448]{0,2,1:T(8,128)}, f32[256,2,448]{0,2,1:T(8,128)})) %all-reduce.11.cloned.1.call-update) | async-done | bytes 1835024 | tf_op jit(solution)/shard_map/psum | solution.py:99
  455.0 3.0 fusion.26
  458.0 1.5 fusion.28
  459.5 1.3 dynamic-slice
  461.5 0.1 select_reduce_fusion.1
  461.6 159.3 %all-reduce.9.cloned.1.call-done = (f32[256,1024]{1,0:T(8,128)}, f32[256,1024]{1,0:T(8,128)}) async-done(((f32[256,1024]{1,0:T(8,128)}, f32[256,1024]{1,0:T(8,128)}), (f32[256,1024]{1,0:T(8,128)}, f32[256,1024]{1,0:T(8,128)})) %all-reduce.9.cloned.1.call-update) | async-done | bytes 2097168
  621.0 0.8 fusion.34
  621.8 0.8 fusion.35
  622.6 0.6 pad_maximum_fusion.4
  (19 shorter events, 0.1 us)
Async XLA Ops:
  6.5 334.5 %copy-start = (bf16[1024,2,448]{0,2,1:T(8,128)(2,1)S(1)}, bf16[1024,2,448]{0,2,1:T(8,128)(2,1)}, u32[]{:S(2)}) copy-start(bf16[1024,2,448]{0,2,1:T(8,128)(2,1)} %param.9) | copy-start | bytes 5505028
  32.3 65.7 %all-to-all-start = ((bf16[64,2,2,8,448]{4,3,2,1,0:T(8,128)(2,1)}), bf16[64,2,2,8,448]{4,3,2,1,0:T(8,128)(2,1)}, u32[]{:S(2)}, u32[]{:S(2)}) async-start(bf16[64,2,2,8,448]{4,3,2,1,0:T(8,128)(2,1)} %pad_maximum_fusion), calls=%async_computation | async-start | bytes 4194304 | tf_op jit(solution)/shard_map/all_to_all | solution.py:35
  59.3 55.8 %copy-start.2 = (bf16[1,2,1024,64]{2,3,1,0:T(8,128)(2,1)S(1)}, bf16[1,2,1024,64]{2,3,1,0:T(8,128)(2,1)}, u32[]{:S(2)}) copy-start(bf16[1,2,1024,64]{2,3,1,0:T(8,128)(2,1)} %param.11) | copy-start | bytes 786436
  98.0 278.5 %all-to-all-start.1 = ((bf16[64,2,2,8,448]{4,3,2,1,0:T(8,128)(2,1)}), bf16[64,2,2,8,448]{4,3,2,1,0:T(8,128)(2,1)}, u32[]{:S(2)}, u32[]{:S(2)}) async-start(bf16[64,2,2,8,448]{4,3,2,1,0:T(8,128)(2,1)} %pad_maximum_fusion.1), calls=%async_computation.2 | async-start | bytes 4194304 | tf_op jit(solution)/shard_map/all_to_all | solution.py:35
  112.5 187.7 %copy-start.1 = (bf16[2,256,1024]{2,1,0:T(8,128)(2,1)S(1)}, bf16[2,256,1024]{2,1,0:T(8,128)(2,1)}, u32[]{:S(2)}) copy-start(bf16[2,256,1024]{2,1,0:T(8,128)(2,1)} %param.8) | copy-start | bytes 3145732
  112.5 187.7 %all-reduce.13.cloned.1.call-start = ((), (), s32[]{:S(2)}) async-start(), calls=%async_computation.8 | async-start | bytes 2097152 | tf_op jit(solution)/shard_map/psum | solution.py:12
  116.2 222.5 %reduce-scatter.3.cloned.1.call-start = ((), (), s32[]{:S(2)}) async-start(), calls=%async_computation.4 | async-start | bytes 147456 | tf_op jit(solution)/shard_map/reduce_scatter | solution.py:82
  300.2 4.3 copy-start.3
  303.3 73.2 %reduce-scatter.5.cloned.1.call-start = ((), (), s32[]{:S(2)}) async-start(), calls=%async_computation.5 | async-start | bytes 147456 | tf_op jit(solution)/shard_map/reduce_scatter | solution.py:82
  305.5 149.5 %all-reduce.11.cloned.1.call-start = ((), (), s32[]{:S(2)}) async-start(), calls=%async_computation.7 | async-start | bytes 3670016 | tf_op jit(solution)/shard_map/psum | solution.py:99
  380.5 77.5 %copy-start.5 = (bf16[448,1024]{1,0:T(8,128)(2,1)S(1)}, bf16[448,1024]{1,0:T(8,128)(2,1)}, u32[]{:S(2)}) copy-start(bf16[448,1024]{1,0:T(8,128)(2,1)} %param.10) | copy-start | bytes 2752516
  380.5 240.5 %all-reduce.9.cloned.1.call-start = ((), (), s32[]{:S(2)}) async-start(), calls=%async_computation.6 | async-start | bytes 4194304
  454.9 3.0 copy-start.6
  458.0 3.5 copy-start.4
Sparse Core Ops, SparseCore 0:
  116.8 183.3 all-reduce.12
  303.4 35.2 reduce-scatter.2
  341.5 34.9 reduce-scatter.4
  380.6 74.3 all-reduce.10
  459.7 161.2 all-reduce.8
where the time goes:
time: 634 us; the launch traced here: 630 us
  waiting for transfers between devices  516 us (81%)
  between operations  34 us (5%)
  starting transfers between devices  32.3 us (5%)
  local copies, waits for them, and re-layouts  20.5 us (3%)
  matrix products  16.2 us (3%)
  other arithmetic  11.1 us (2%)
    psum x1, waiting for transfers between devices, from_root(): return lax.psum(jnp.where(mine, shard, jnp.zeros_like(shard)), axis)  176 us
    unnamed x6, waiting for transfers between devices  159 us
    psum x1, waiting for transfers between devices, shards(): totals = lax.psum(partial_sums, 'tensor')  74.4 us
    reduce_scatter x2, waiting for transfers between devices, shards(): lax.psum_scatter(shrunk, 'tensor', scatter_dimension=2, tiled=True)  66.9 us
    all_to_all x2, waiting for transfers between devices, fetch_split(): lax.all_to_all(jnp.stack(outgoing, axis=1), 'pool', split_axis=0, concat_...  38.6 us
    all_to_all x2, starting transfers between devices, fetch_split(): lax.all_to_all(jnp.stack(outgoing, axis=1), 'pool', split_axis=0, concat_...  31.9 us
  transfers between devices with their start and end apart: 7, of which 6 were waited for; matrix products, arithmetic and copies ran while one was open for 3% of the time, Pallas kernels for 0%

commit v1 on v0

v1 whole, which is shorter than its diff:
```python
import functools

import jax
import jax.numpy as jnp
from jax import lax
from jax.experimental import pallas as pl
from jax.experimental.pallas import tpu as pltpu
from jax.sharding import PartitionSpec as P

NBLK = 2
STEPS = 2
NSB = STEPS * NBLK
WIN = 512
MESH = pl.DeviceIdType.MESH
F32 = jnp.float32
BF16 = jnp.bfloat16


class Exchange:
    def __init__(self, ssem, rsem, phase, n, me, dev):
        self.ssem, self.rsem, self.phase = ssem, rsem, phase
        self.n, self.me, self.dev = n, me, dev

    def copy(self, k, src, dst, source):
        peer = lax.rem(self.me + k, self.n)
        return pltpu.make_async_remote_copy(
            src_ref=src(peer),
            dst_ref=dst(source),
            send_sem=self.ssem.at[self.phase, k],
            recv_sem=self.rsem.at[self.phase, source],
            device_id=self.dev(peer),
            device_id_type=MESH,
        )

    def start(self, src, dst):
        self.src, self.dst = src, dst
        for k in range(1, self.n):
            self.copy(k, src, dst, self.me).start()

    def wait_recv(self):
        for k in range(1, self.n):
            self.copy(k, self.src, self.dst, lax.rem(self.me + k, self.n)).wait_recv()

    def wait_send(self):
        for k in range(1, self.n):
            self.copy(k, self.src, self.dst, self.me).wait_send()


def nt(a, b):
    return lax.dot_general(a, b, (((1,), (1,)), ((), ())), preferred_element_type=F32)


def kernel(
    ny, nz, block,
    adapter_ref, live_ref, slot_ref, tok_h, w_h, s_h, e_h, d_h, out_ref,
    tok, w, sh, ev, dn,
    sp, srx, sy, sz, pb, brx,
    e1y, e1z, sel0, sel1, e2y, e2z, ets, erx, ecat,
    hid, o0, o1, r0, r1, acc0, acc1, q0, q1, u0, u1,
    ssem, rsem, lsem,
):
    nt_ = lax.axis_size("tensor")
    p = lax.axis_index("pool")
    t = lax.axis_index("tensor")
    y = lax.div(p, nz)
    z = lax.rem(p, nz)
    rows_t = tok.shape[0] // nt_
    ranks = s_h.shape[1]
    units = w_h.shape[1]
    step_rows = tok.shape[0] // STEPS
    grp = step_rows // (ny * nz)
    span = nz * units
    zshift = nz.bit_length() - 1

    def ydev(i):
        return (i * nz + z, t)

    def zdev(i):
        return (y * nz + i, t)

    def tdev(i):
        return (p, i)

    def win(zi):
        return pl.multiple_of(lax.div(zi * units, 128) * 128, 128)

    barrier = pltpu.get_barrier_semaphore()
    for n, me, dev in ((ny, y, ydev), (nz, z, zdev), (nt_, t, tdev)):
        for k in range(1, n):
            pl.semaphore_signal(
                barrier, inc=1, device_id=dev(lax.rem(me + k, n)), device_id_type=MESH
            )

    loads = [
        pltpu.make_async_copy(s_h.at[0], sh.at[pl.ds(0, ranks)], lsem.at[0]),
        pltpu.make_async_copy(s_h.at[1], sh.at[pl.ds(ranks, ranks)], lsem.at[1]),
        pltpu.make_async_copy(tok_h, tok, lsem.at[2]),
        pltpu.make_async_copy(w_h, w, lsem.at[3]),
        pltpu.make_async_copy(d_h, dn, lsem.at[4]),
        pltpu.make_async_copy(
            e_h.at[0, :, pl.ds(pl.multiple_of(y * span, 128), span)], e1y.at[y], lsem.at[5]
        ),
    ]
    ecopies = [
        pltpu.make_async_copy(
            e_h.at[1, :, pl.ds(i * span, span)], ev.at[i], lsem.at[6 + i]
        )
        for i in range(ny)
    ]
    for c in ecopies + loads:
        c.start()

    exch = functools.partial(Exchange, ssem, rsem)
    x_e1y = exch(0, ny, y, ydev)
    x_e1z = exch(1, nz, z, zdev)
    x_s = exch(2, nt_, t, tdev)
    x_b = [exch(3, nt_, t, tdev), exch(4, nt_, t, tdev)]
    x_sy = exch(5, ny, y, ydev)
    x_sz = exch(6, nz, z, zdev)
    x_e2y = exch(7, nz, z, zdev)
    x_e2z = exch(8, ny, y, ydev)
    x_et = exch(9, nt_, t, tdev)
    x_h = exch(10, nt_, t, tdev)
    x_o0 = exch(11, ny, y, ydev)
    x_o1 = exch(12, nz, z, zdev)
    x_q0 = exch(13, nz, z, zdev)
    x_q1 = exch(14, ny, y, ydev)

    for c in ecopies:
        c.wait()
    pl.semaphore_wait(barrier, (ny - 1) + (nz - 1) + (nt_ - 1))

    x_e1y.start(
        lambda i: e_h.at[0, :, pl.ds(pl.multiple_of(i * span, 128), span)],
        lambda m: e1y.at[m],
    )
    x_e1z.start(lambda i: ev.at[:, :, pl.ds(win(i), WIN)], lambda m: e1z.at[m])
    own_z = pltpu.make_async_copy(
        ev.at[:, :, pl.ds(win(z), WIN)], e1z.at[z], lsem.at[6 + ny]
    )
    own_z.start()

    for c in loads[:3]:
        c.wait()
    s_part = nt(tok[...], sh[...]).astype(BF16)
    for i in range(nt_):
        sp[i] = s_part[i * rows_t:(i + 1) * rows_t]
    x_s.start(lambda i: sp.at[i], lambda m: srx.at[m])

    loads[3].wait()

    def base(k):
        part = nt(tok[...], w[k]).astype(BF16)
        for i in range(nt_):
            pb[k, i] = part[i * rows_t:(i + 1) * rows_t]
        x_b[k].start(lambda i: pb.at[k, i], lambda m: brx.at[k, m])

    base(0)

    x_s.wait_recv()
    total = sp[t].astype(F32)
    for k in range(1, nt_):
        total = total + srx[lax.rem(t + k, nt_)].astype(F32)
    sy[y] = total.astype(BF16)
    x_sy.start(lambda i: sy.at[y], lambda m: sy.at[m])

    base(1)

    slots = [slot_ref[adapter_ref[i // NBLK, i % NBLK]] for i in range(NSB)]
    yo = [lax.shift_right_logical(s, zshift) for s in slots]
    zo = [lax.bitwise_and(s, nz - 1) for s in slots]
    mine = lax.div(t * rows_t, block)
    my_slot = slot_ref[adapter_ref[lax.div(mine, NBLK), lax.rem(mine, NBLK)]]
    my_yo = lax.shift_right_logical(my_slot, zshift)
    my_zo = lax.bitwise_and(my_slot, nz - 1)

    x_sy.wait_recv()
    sz[z] = sy[my_yo]
    x_sz.start(lambda i: sz.at[z], lambda m: sz.at[m])

    loads[5].wait()
    x_e1y.wait_recv()
    for i in range(NSB):
        sel0[i] = e1y[yo[i]]
    x_e2y.start(lambda i: sel0.at[:, :, pl.ds(win(i), WIN)], lambda m: e2y.at[m])
    e2y[z] = sel0[:, :, pl.ds(win(z), WIN)]
    own_z.wait()
    x_e1z.wait_recv()
    for i in range(NSB):
        sel1[i] = e1z[zo[i]]
    x_e2z.start(lambda i: sel1.at[:, i], lambda m: e2z.at[m])
    e2z[y] = sel1[:, y]

    sums = []
    for k in range(2):
        x_b[k].wait_recv()
        total = pb[k, t].astype(F32)
        for j in range(1, nt_):
            total = total + brx[k, lax.rem(t + j, nt_)].astype(F32)
        sums.append(total)

    x_sz.wait_recv()
    shrunk = sz[my_zo]

    x_e2y.wait_recv()
    for i in range(NSB):
        ets[i, 0] = e2y[zo[i], i]
    x_e2z.wait_recv()
    for i in range(NSB):
        ets[i, 1] = e2z[yo[i], i]
    x_et.start(lambda i: ets.at[lax.div(i * rows_t, block)], lambda m: erx.at[m])
    erx[t] = ets[mine]
    x_et.wait_recv()
    rank_t = ranks // nt_
    for k in range(2):
        for i in range(nt_):
            ecat[pl.ds(k * ranks + i * rank_t, rank_t)] = erx[i, k].astype(F32)
    second = ecat[...]
    rolled = pltpu.roll(second, WIN - 64, axis=1)
    odd = lax.rem(z, 2) == 1
    second = jnp.where(odd, rolled, second).astype(BF16)
    lane = lax.broadcasted_iota(jnp.int32, shrunk.shape, 1)
    zero = jnp.zeros_like(shrunk)
    gate = jnp.dot(jnp.where(lane < ranks, shrunk, zero), second, preferred_element_type=F32)
    up = jnp.dot(jnp.where(lane < ranks, zero, shrunk), second, preferred_element_type=F32)
    gate = sums[0] + gate[:, :units]
    up = sums[1] + up[:, :units]
    hid[t] = (gate / (1.0 + jnp.exp(-gate)) * up).astype(BF16)
    x_h.start(lambda i: hid.at[t], lambda m: hid.at[m])
    loads[4].wait()
    x_h.wait_recv()

    half = nt_ // STEPS
    h0 = hid[0:half].reshape(step_rows, units)
    part = jnp.dot(h0, dn[...], preferred_element_type=F32).astype(BF16)
    for i in range(ny):
        o0[i] = part[i * nz * grp:(i + 1) * nz * grp]
    x_o0.start(lambda i: o0.at[i], lambda m: r0.at[m])

    h1 = hid[half:nt_].reshape(step_rows, units)
    ri = lax.broadcasted_iota(jnp.int32, (step_rows, step_rows), 0)
    ci = lax.broadcasted_iota(jnp.int32, (step_rows, step_rows), 1)
    gbits = grp.bit_length() - 1
    ybits = ny.bit_length() - 1
    low = lax.bitwise_and(ri, grp - 1)
    yy = lax.bitwise_and(lax.shift_right_logical(ri, gbits), ny - 1)
    zz = lax.shift_right_logical(ri, gbits + ybits)
    perm = jnp.where(ci == yy * (nz * grp) + zz * grp + low, 1.0, 0.0).astype(BF16)
    h1 = jnp.dot(perm, h1, preferred_element_type=F32).astype(BF16)
    part = jnp.dot(h1, dn[...], preferred_element_type=F32).astype(BF16)
    for i in range(nz):
        o1[i] = part[i * ny * grp:(i + 1) * ny * grp]
    x_o1.start(lambda i: o1.at[i], lambda m: r1.at[m])

    x_o0.wait_recv()
    total = o0[y].astype(F32)
    for k in range(1, ny):
        total = total + r0[lax.rem(y + k, ny)].astype(F32)
    acc0[...] = total
    for i in range(nz):
        q0[i] = acc0[pl.ds(i * grp, grp), :]
    x_q0.start(lambda i: q0.at[i], lambda m: u0.at[m])

    x_o1.wait_recv()
    total = o1[z].astype(F32)
    for k in range(1, nz):
        total = total + r1[lax.rem(z + k, nz)].astype(F32)
    acc1[...] = total
    for i in range(ny):
        q1[i] = acc1[pl.ds(i * grp, grp), :]
    x_q1.start(lambda i: q1.at[i], lambda m: u1.at[m])

    first = p * grp
    place = lax.rem(first, block) + lax.broadcasted_iota(jnp.int32, q0.shape[1:], 0)
    owner = lax.div(first, block)
    for step, (x, q, u, n, me) in enumerate(
        ((x_q0, q0, u0, nz, z), (x_q1, q1, u1, ny, y))
    ):
        x.wait_recv()
        total = q[me]
        for k in range(1, n):
            total = total + u[lax.rem(me + k, n)]
        keep = place < live_ref[step, owner]
        out_ref[step] = jnp.where(keep, total, 0.0).astype(BF16)

    for x in (x_e1y, x_e1z, x_s, *x_b, x_sy, x_sz, x_e2y, x_e2z, x_et, x_h,
              x_o0, x_o1, x_q0, x_q1):
        x.wait_send()


def shards(ny, nz, block, tokens, gate_up, down, shrink, expand, adapter, live, slots):
    steps, rows, width = tokens.shape
    units = gate_up.shape[2]
    ranks = shrink.shape[3]
    rank_t = expand.shape[2]
    n_t = lax.axis_size("tensor")
    rows_t = steps * rows // n_t
    grp = rows // (ny * nz)
    span = nz * units
    any_spec = pl.BlockSpec(memory_space=pl.ANY)
    smem = pl.BlockSpec(memory_space=pltpu.SMEM)
    vmem = pltpu.VMEM
    scratch = [
        vmem((steps * rows, width), BF16),
        vmem((2, units, width), BF16),
        vmem((2 * ranks, width), BF16),
        vmem((ny, rank_t, span), BF16),
        vmem((units, width), BF16),
        vmem((n_t, rows_t, 2 * ranks), BF16),
        vmem((n_t, rows_t, 2 * ranks), BF16),
        vmem((ny, rows_t, 2 * ranks), BF16),
        vmem((nz, rows_t, 2 * ranks), BF16),
        vmem((2, n_t, rows_t, units), BF16),
        vmem((2, n_t, rows_t, units), BF16),
        vmem((ny, rank_t, span), BF16),
        vmem((nz, ny, rank_t, WIN), BF16),
        vmem((NSB, rank_t, span), BF16),
        vmem((NSB, ny, rank_t, WIN), BF16),
        vmem((nz, NSB, rank_t, WIN), BF16),
        vmem((ny, NSB, rank_t, WIN), BF16),
        vmem((NSB, 2, rank_t, WIN), BF16),
        vmem((n_t, 2, rank_t, WIN), BF16),
        vmem((2 * ranks, WIN), F32),
        vmem((n_t, rows_t, units), BF16),
        vmem((ny, nz * grp, width), BF16),
        vmem((nz, ny * grp, width), BF16),
        vmem((ny, nz * grp, width), BF16),
        vmem((nz, ny * grp, width), BF16),
        vmem((nz * grp, width), F32),
        vmem((ny * grp, width), F32),
        vmem((nz, grp, width), F32),
        vmem((ny, grp, width), F32),
        vmem((nz, grp, width), F32),
        vmem((ny, grp, width), F32),
        pltpu.SemaphoreType.DMA((15, max(ny, nz, n_t))),
        pltpu.SemaphoreType.DMA((15, max(ny, nz, n_t))),
        pltpu.SemaphoreType.DMA((7 + ny,)),
    ]
    return pl.pallas_call(
        functools.partial(kernel, ny, nz, block),
        out_shape=jax.ShapeDtypeStruct((steps, grp, width), BF16),
        in_specs=[smem, smem, smem] + [any_spec] * 5,
        out_specs=pl.BlockSpec(memory_space=pltpu.VMEM),
        scratch_shapes=scratch,
        compiler_params=pltpu.CompilerParams(collective_id=0, has_side_effects=True),
        name="layer",
    )(
        adapter,
        live,
        slots,
        tokens.reshape(steps * rows, width),
        gate_up.transpose(1, 2, 0),
        shrink[0].transpose(0, 2, 1),
        expand[0],
        down,
    )


def build(mesh, ny, nz, block):
    return jax.shard_map(
        functools.partial(shards, ny, nz, block),
        mesh=mesh,
        in_specs=(
            P(None, None, "tensor"),
            P("tensor", None, "pool"),
            P("pool", "tensor"),
            P("pool", None, "tensor", None),
            P("pool", None, "tensor", None),
            P(),
            P(),
            P(),
        ),
        out_specs=P(None, "pool", "tensor"),
        check_vma=False,
    )


def solution(mesh):
    return build(mesh, 8, 8, 128)
```

time: 634 us -> 80.5 us (0.13)
  waiting for transfers between devices: 516 us -> 0 us
  Pallas kernels: 0 us -> 79 us
  between operations: 34 us -> 0.01 us
  starting transfers between devices: 32.3 us -> 0 us
  local copies, waits for them, and re-layouts: 20.5 us -> 1.33 us
  matrix products: 16.2 us -> 0 us
  other arithmetic: 11.1 us -> 0 us
    psum x2 -> x0, waiting for transfers between devices: 251 us -> none  [the longest x1 176 us: from_root(): return lax.psum(jnp.where(mine, shard, jnp.zeros_like(shard)), axis)]
    unnamed x6 -> x0, waiting for transfers between devices: 159 us -> none
    pallas_call x0 -> x1, Pallas kernels: none -> 79 us  [shards(): pl.pallas_call(functools.partial(kernel, ny, nz, block), out_shape=jax.Sh...]
    reduce_scatter x2 -> x0, waiting for transfers between devices: 66.9 us -> none  [shards(): lax.psum_scatter(shrunk, 'tensor', scatter_dimension=2, tiled=True)]
    all_to_all x2 -> x0, waiting for transfers between devices: 38.6 us -> none  [fetch_split(): lax.all_to_all(jnp.stack(outgoing, axis=1), 'pool', split_axis=0, concat_...]
    all_to_all x2 -> x0, starting transfers between devices: 31.9 us -> none  [fetch_split(): lax.all_to_all(jnp.stack(outgoing, axis=1), 'pool', split_axis=0, concat_...]
    dot_general x12 -> x0, matrix products: 16.2 us -> none  [the longest x4 4.55 us: shards(): jnp.einsum('knc,kcf->nkf', rank_share[:, block_index * BLK:(block_index +...]
    mul x5 -> x0, local copies, waits for them, and re-layouts: 11.5 us -> none  [the longest x4 11.5 us: fetch_split(): outgoing.append(split_cols * mine)]
  transfers between devices with their start and end apart: 7 -> 0, of which waited for: 6 -> 0; matrix products, arithmetic and copies ran while one was open for 3% -> 0% of each run, Pallas kernels for 0% -> 0%
where the time goes in v1:
time: 80.5 us; the launch traced here: 80.3 us
  Pallas kernels  79 us (98%)
  local copies, waits for them, and re-layouts  1.33 us (2%)
    pallas_call x1, Pallas kernels, shards(): pl.pallas_call(functools.partial(kernel, ny, nz, block), out_shape=jax.Sh...  79 us

profile of v1, /device:TPU:1, one launch (start us, length us, event | category | flops | bytes accessed | tf_op | source)
XLA Modules:
  0.0 80.3 jit_solution(7337066005532979132)
XLA Ops:
  0.0 79.0 %layer.1 = bf16[2,4,1024]{2,1,0:T(4,128)(2,1)} custom-call(s32[2,2]{1,0:T(2,128)} %adapter_ref.1, s32[2,2]{1,0:T(2,128)} %live_ref.1, s32[64]{0:T(128)} %slot_ref.1, bf16[512,1024]{1,0:T(8,128)(2,1)} %bitcast.7, bf16[2,448,1024]{2,1,0:T(8,128)(2,1)} %bitcast.6, bf16[2,64,1024]{2,1,0:T(8,128)(2,1)} %bitcast.9, bf16[2,8,28672]{2,1,0:T(8,128)(2,1)} %bitcast.8, ...), custom_call_target="tpu_custom_call" | custom-call | tf_op jit(solution)/shard_map/layer/pallas_call | solution.py:339
  79.0 1.3 %copy.10 = bf16[2,4,1024]{2,1,0:T(4,128)(2,1)} copy(bf16[2,4,1024]{2,1,0:T(4,128)(2,1)} %layer.1) | data formatting | bytes 32768

commit v2 on v1

v2 whole, which is shorter than its diff:
```python
import functools

import jax
import jax.numpy as jnp
from jax import lax
from jax.experimental import pallas as pl
from jax.experimental.pallas import tpu as pltpu
from jax.sharding import PartitionSpec as P

NBLK = 2
STEPS = 2
NSB = STEPS * NBLK
CORES = 2
WIN = 512
MESH = pl.DeviceIdType.MESH
F32 = jnp.float32
BF16 = jnp.bfloat16


class Exchange:
    def __init__(self, ssem, rsem, phase, me, peers, dev):
        self.ssem, self.rsem, self.phase = ssem, rsem, phase
        self.me, self.peers, self.dev = me, peers, dev

    def copy(self, peer, src, dst, source):
        return pltpu.make_async_remote_copy(
            src_ref=src(peer),
            dst_ref=dst(source),
            send_sem=self.ssem.at[self.phase, peer],
            recv_sem=self.rsem.at[self.phase, source],
            device_id=self.dev(peer),
            device_id_type=MESH,
        )

    def start(self, src, dst):
        self.src, self.dst = src, dst
        for peer in self.peers:
            self.copy(peer, src, dst, self.me).start()

    def wait_from(self, peer):
        self.copy(peer, self.src, self.dst, peer).wait_recv()

    def wait_recv(self):
        for peer in self.peers:
            self.wait_from(peer)

    def wait_send(self):
        for peer in self.peers:
            self.copy(peer, self.src, self.dst, self.me).wait_send()


def nt(a, b):
    return lax.dot_general(a, b, (((1,), (1,)), ((), ())), preferred_element_type=F32)


def kernel(
    ny, nz, block,
    adapter_ref, live_ref, slot_ref, tok_h, w_h, s_h, e_h, d_h, out_ref,
    tok, w, sh, ev, dn,
    sp, srx, sy, sz, pb, brx,
    e1y, e1z, sel0, sel1, e2y, e2z, ets, erx, ecat,
    hid, o0, o1, r0, r1, acc0, acc1, q0, q1, u0, u1,
    ssem, rsem, lsem, os0, or0, os1, or1,
):
    nt_ = lax.axis_size("tensor")
    p = lax.axis_index("pool")
    t = lax.axis_index("tensor")
    y = lax.div(p, nz)
    z = lax.rem(p, nz)
    rows_t = tok.shape[0] // nt_
    ranks = s_h.shape[1]
    units = w_h.shape[1]
    step_rows = tok.shape[0] // STEPS
    grp = step_rows // (ny * nz)
    span = nz * units
    zshift = nz.bit_length() - 1

    nx = nt_ // CORES
    x = lax.div(t, CORES)
    core = lax.rem(t, CORES)
    width = dn.shape[1]
    hw = width // 2
    hops = [0] + sorted(range(1, nx), key=lambda d: min(d, nx - d))
    chips = [lax.rem(x + d, nx) for d in hops]
    ypeers = [lax.rem(y + k, ny) for k in range(1, ny)]
    zpeers = [lax.rem(z + k, nz) for k in range(1, nz)]
    other = CORES * x + (CORES - 1 - core)
    tpeers = [other] + [
        CORES * c + lax.rem(core + i, CORES) for c in chips[1:] for i in range(CORES)
    ]

    def ydev(i):
        return (i * nz + z, t)

    def zdev(i):
        return (y * nz + i, t)

    def tdev(i):
        return (p, i)

    def win(zi):
        return pl.multiple_of(lax.div(zi * units, 128) * 128, 128)

    barrier = pltpu.get_barrier_semaphore()
    for peers, dev in ((ypeers, ydev), (zpeers, zdev), (tpeers, tdev)):
        for i in peers:
            pl.semaphore_signal(barrier, inc=1, device_id=dev(i), device_id_type=MESH)

    loads = [
        pltpu.make_async_copy(s_h.at[0], sh.at[pl.ds(0, ranks)], lsem.at[0]),
        pltpu.make_async_copy(s_h.at[1], sh.at[pl.ds(ranks, ranks)], lsem.at[1]),
        pltpu.make_async_copy(tok_h, tok, lsem.at[2]),
        pltpu.make_async_copy(w_h, w, lsem.at[3]),
        pltpu.make_async_copy(d_h, dn, lsem.at[4]),
        pltpu.make_async_copy(
            e_h.at[0, :, pl.ds(pl.multiple_of(y * span, 128), span)], e1y.at[y], lsem.at[5]
        ),
    ]
    ecopies = [
        pltpu.make_async_copy(
            e_h.at[1, :, pl.ds(i * span, span)], ev.at[i], lsem.at[6 + i]
        )
        for i in range(ny)
    ]
    for c in ecopies + loads:
        c.start()

    def on_y(phase):
        return Exchange(ssem, rsem, phase, y, ypeers, ydev)

    def on_z(phase):
        return Exchange(ssem, rsem, phase, z, zpeers, zdev)

    def on_t(phase):
        return Exchange(ssem, rsem, phase, t, tpeers, tdev)

    x_e1y, x_e1z = on_y(0), on_z(1)
    x_s, x_sy, x_sz = on_t(2), on_y(3), on_z(4)
    x_b = [on_t(5), on_t(6)]
    x_e2y, x_e2z, x_et = on_z(7), on_y(8), on_t(9)
    x_h = on_t(10)
    x_q0, x_q1 = on_z(11), on_y(12)

    for c in ecopies:
        c.wait()
    pl.semaphore_wait(barrier, (ny - 1) + (nz - 1) + (nt_ - 1))

    x_e1y.start(
        lambda i: e_h.at[0, :, pl.ds(pl.multiple_of(i * span, 128), span)],
        lambda m: e1y.at[m],
    )
    x_e1z.start(lambda i: ev.at[:, :, pl.ds(win(i), WIN)], lambda m: e1z.at[m])
    own_z = pltpu.make_async_copy(
        ev.at[:, :, pl.ds(win(z), WIN)], e1z.at[z], lsem.at[6 + ny]
    )
    own_z.start()

    for c in loads[:3]:
        c.wait()
    s_part = nt(tok[...], sh[...])
    for i in range(nt_):
        sp[i] = s_part[i * rows_t:(i + 1) * rows_t]
    x_s.start(lambda i: sp.at[i], lambda m: srx.at[m])

    loads[3].wait()

    def base(k):
        part = nt(tok[...], w[k]).astype(BF16)
        for i in range(nt_):
            pb[k, i] = part[i * rows_t:(i + 1) * rows_t]
        x_b[k].start(lambda i: pb.at[k, i], lambda m: brx.at[k, m])

    base(0)

    x_s.wait_recv()
    total = sp[t]
    for i in tpeers:
        total = total + srx[i]
    sy[y] = total.astype(BF16)
    x_sy.start(lambda i: sy.at[y], lambda m: sy.at[m])

    base(1)

    slots = [slot_ref[adapter_ref[i // NBLK, i % NBLK]] for i in range(NSB)]
    yo = [lax.shift_right_logical(s, zshift) for s in slots]
    zo = [lax.bitwise_and(s, nz - 1) for s in slots]
    mine = lax.div(t * rows_t, block)
    my_slot = slot_ref[adapter_ref[lax.div(mine, NBLK), lax.rem(mine, NBLK)]]
    my_yo = lax.shift_right_logical(my_slot, zshift)
    my_zo = lax.bitwise_and(my_slot, nz - 1)

    loads[5].wait()
    x_e1y.wait_recv()
    for i in range(NSB):
        sel0[i] = e1y[yo[i]]
    x_e2y.start(lambda i: sel0.at[:, :, pl.ds(win(i), WIN)], lambda m: e2y.at[m])
    own_z.wait()
    x_e1z.wait_recv()
    for i in range(NSB):
        sel1[i] = e1z[zo[i]]
    x_e2z.start(lambda i: sel1.at[:, i], lambda m: e2z.at[m])
    x_sy.wait_recv()
    sz[z] = sy[my_yo]
    x_sz.start(lambda i: sz.at[z], lambda m: sz.at[m])
    e2y[z] = sel0[:, :, pl.ds(win(z), WIN)]
    e2z[y] = sel1[:, y]

    sums = []
    for k in range(2):
        x_b[k].wait_recv()
        total = pb[k, t].astype(F32)
        for i in tpeers:
            total = total + brx[k, i].astype(F32)
        sums.append(total)

    x_e2y.wait_recv()
    for i in range(NSB):
        ets[i, 0] = e2y[zo[i], i]
    x_e2z.wait_recv()
    for i in range(NSB):
        ets[i, 1] = e2z[yo[i], i]
    x_et.start(lambda i: ets.at[lax.div(i * rows_t, block)], lambda m: erx.at[m])
    erx[t] = ets[mine]
    x_sz.wait_recv()
    shrunk = sz[my_zo]
    x_et.wait_recv()
    rank_t = ranks // nt_
    for k in range(2):
        for i in range(nt_):
            ecat[pl.ds(k * ranks + i * rank_t, rank_t)] = erx[i, k].astype(F32)
    second = ecat[...]
    rolled = pltpu.roll(second, WIN - 64, axis=1)
    odd = lax.rem(z, 2) == 1
    second = jnp.where(odd, rolled, second).astype(BF16)
    lane = lax.broadcasted_iota(jnp.int32, shrunk.shape, 1)
    zero = jnp.zeros_like(shrunk)
    gate = jnp.dot(jnp.where(lane < ranks, shrunk, zero), second, preferred_element_type=F32)
    up = jnp.dot(jnp.where(lane < ranks, zero, shrunk), second, preferred_element_type=F32)
    gate = sums[0] + gate[:, :units]
    up = sums[1] + up[:, :units]
    hid[t] = (gate / (1.0 + jnp.exp(-gate)) * up).astype(BF16)
    x_h.start(lambda i: hid.at[t], lambda m: hid.at[m])
    loads[4].wait()

    gps = nx // STEPS
    ypg = ny // gps
    rows_g = CORES * rows_t
    part_y = nz * grp
    part_z = ypg * grp
    ri = lax.broadcasted_iota(jnp.int32, (rows_g, rows_g), 0)
    ci = lax.broadcasted_iota(jnp.int32, (rows_g, rows_g), 1)
    gbits = grp.bit_length() - 1
    ybits = ypg.bit_length() - 1
    low = lax.bitwise_and(ri, grp - 1)
    yy = lax.bitwise_and(lax.shift_right_logical(ri, gbits), ypg - 1)
    zz = lax.shift_right_logical(ri, gbits + ybits)
    perm = jnp.where(ci == yy * part_y + zz * grp + low, 1.0, 0.0).astype(BF16)

    def copy_y(peer, source, step):
        return pltpu.make_async_remote_copy(
            src_ref=o0.at[peer, step],
            dst_ref=r0.at[source, step],
            send_sem=os0.at[peer, step],
            recv_sem=or0.at[source, step],
            device_id=ydev(peer),
            device_id_type=MESH,
        )

    def copy_z(peer, source, chip):
        return pltpu.make_async_remote_copy(
            src_ref=o1.at[peer, chip],
            dst_ref=r1.at[source, chip],
            send_sem=os1.at[peer, chip],
            recv_sem=or1.at[source, chip],
            device_id=zdev(peer),
            device_id_type=MESH,
        )

    for j, chip in enumerate(chips):
        for i in tpeers[:1] if j == 0 else tpeers[CORES * j - 1:CORES * j + 1]:
            x_h.wait_from(i)
        h = hid[pl.ds(CORES * chip, CORES)].reshape(rows_g, units)
        step = lax.div(chip, gps)
        first = lax.rem(chip, gps) * ypg
        part = jnp.dot(h, dn[:, :hw], preferred_element_type=F32).astype(BF16)
        for i in range(ypg):
            o0[first + i, step] = part[i * part_y:(i + 1) * part_y]
        for i in range(ypg):
            peer = first + lax.rem(y + i, ypg)

            @pl.when(peer != y)
            def _(peer=peer, step=step):
                copy_y(peer, y, step).start()

        h = jnp.dot(perm, h, preferred_element_type=F32).astype(BF16)
        part = jnp.dot(h, dn[:, hw:], preferred_element_type=F32).astype(BF16)
        for i in range(nz):
            o1[i, chip] = part[i * part_z:(i + 1) * part_z]
        for peer in zpeers:
            copy_z(peer, z, chip).start()

    total = o0[y].astype(F32)
    for i in ypeers:
        for step in range(STEPS):
            copy_y(i, i, step).wait_recv()
        total = total + r0[i].astype(F32)
    acc0[...] = total
    for i in range(nz):
        q0[i] = acc0[:, pl.ds(i * grp, grp), :]
    x_q0.start(lambda i: q0.at[i], lambda m: u0.at[m])

    total = o1[z].astype(F32)
    for i in zpeers:
        for chip in range(nx):
            copy_z(i, i, chip).wait_recv()
        total = total + r1[i].astype(F32)
    acc1[...] = total.reshape(STEPS, ny * grp, hw)
    for i in range(ny):
        q1[i] = acc1[:, pl.ds(i * grp, grp), :]
    x_q1.start(lambda i: q1.at[i], lambda m: u1.at[m])

    first = p * grp
    place = lax.rem(first, block) + lax.broadcasted_iota(jnp.int32, (grp, hw), 0)
    owner = lax.div(first, block)
    for half, (xq, q, u, peers, me) in enumerate(
        ((x_q0, q0, u0, zpeers, z), (x_q1, q1, u1, ypeers, y))
    ):
        total = q[me]
        for i in peers:
            xq.wait_from(i)
            total = total + u[i]
        for step in range(STEPS):
            keep = place < live_ref[step, owner]
            out_ref[step, :, half * hw:(half + 1) * hw] = jnp.where(
                keep, total[step], 0.0
            ).astype(BF16)

    for e in (x_e1y, x_e1z, x_s, *x_b, x_sy, x_sz, x_e2y, x_e2z, x_et, x_h, x_q0, x_q1):
        e.wait_send()
    for i in ypeers:
        for step in range(STEPS):
            copy_y(i, y, step).wait_send()
    for i in zpeers:
        for chip in range(nx):
            copy_z(i, z, chip).wait_send()


def shards(ny, nz, block, tokens, gate_up, down, shrink, expand, adapter, live, slots):
    steps, rows, width = tokens.shape
    units = gate_up.shape[2]
    ranks = shrink.shape[3]
    rank_t = expand.shape[2]
    n_t = lax.axis_size("tensor")
    rows_t = steps * rows // n_t
    grp = rows // (ny * nz)
    span = nz * units
    hw = width // 2
    nx = n_t // CORES
    part_z = ny // (nx // steps) * grp
    any_spec = pl.BlockSpec(memory_space=pl.ANY)
    smem = pl.BlockSpec(memory_space=pltpu.SMEM)
    vmem = pltpu.VMEM
    scratch = [
        vmem((steps * rows, width), BF16),
        vmem((2, units, width), BF16),
        vmem((2 * ranks, width), BF16),
        vmem((ny, rank_t, span), BF16),
        vmem((units, width), BF16),
        vmem((n_t, rows_t, 2 * ranks), F32),
        vmem((n_t, rows_t, 2 * ranks), F32),
        vmem((ny, rows_t, 2 * ranks), BF16),
        vmem((nz, rows_t, 2 * ranks), BF16),
        vmem((2, n_t, rows_t, units), BF16),
        vmem((2, n_t, rows_t, units), BF16),
        vmem((ny, rank_t, span), BF16),
        vmem((nz, ny, rank_t, WIN), BF16),
        vmem((NSB, rank_t, span), BF16),
        vmem((NSB, ny, rank_t, WIN), BF16),
        vmem((nz, NSB, rank_t, WIN), BF16),
        vmem((ny, NSB, rank_t, WIN), BF16),
        vmem((NSB, 2, rank_t, WIN), BF16),
        vmem((n_t, 2, rank_t, WIN), BF16),
        vmem((2 * ranks, WIN), F32),
        vmem((n_t, rows_t, units), BF16),
        vmem((ny, steps, nz * grp, hw), BF16),
        vmem((nz, nx, part_z, hw), BF16),
        vmem((ny, steps, nz * grp, hw), BF16),
        vmem((nz, nx, part_z, hw), BF16),
        vmem((steps, nz * grp, hw), F32),
        vmem((steps, ny * grp, hw), F32),
        vmem((nz, steps, grp, hw), F32),
        vmem((ny, steps, grp, hw), F32),
        vmem((nz, steps, grp, hw), F32),
        vmem((ny, steps, grp, hw), F32),
        pltpu.SemaphoreType.DMA((13, max(ny, nz, n_t))),
        pltpu.SemaphoreType.DMA((13, max(ny, nz, n_t))),
        pltpu.SemaphoreType.DMA((7 + ny,)),
        pltpu.SemaphoreType.DMA((ny, steps)),
        pltpu.SemaphoreType.DMA((ny, steps)),
        pltpu.SemaphoreType.DMA((nz, nx)),
        pltpu.SemaphoreType.DMA((nz, nx)),
    ]
    return pl.pallas_call(
        functools.partial(kernel, ny, nz, block),
        out_shape=jax.ShapeDtypeStruct((steps, grp, width), BF16),
        in_specs=[smem, smem, smem] + [any_spec] * 5,
        out_specs=pl.BlockSpec(memory_space=pltpu.VMEM),
        scratch_shapes=scratch,
        compiler_params=pltpu.CompilerParams(collective_id=0, has_side_effects=True),
        name="layer",
    )(
        adapter,
        live,
        slots,
        tokens.reshape(steps * rows, width),
        gate_up.transpose(1, 2, 0),
        shrink[0].transpose(0, 2, 1),
        expand[0],
        down,
    )


def build(mesh, ny, nz, block):
    return jax.shard_map(
        functools.partial(shards, ny, nz, block),
        mesh=mesh,
        in_specs=(
            P(None, None, "tensor"),
            P("tensor", None, "pool"),
            P("pool", "tensor"),
            P("pool", None, "tensor", None),
            P("pool", None, "tensor", None),
            P(),
            P(),
            P(),
        ),
        out_specs=P(None, "pool", "tensor"),
        check_vma=False,
    )


def solution(mesh):
    return build(mesh, 8, 8, 128)
```

time: 80.5 us -> 71.7 us (0.89)
  Pallas kernels: 79 us -> 70.2 us
    pallas_call x1, Pallas kernels: 79 us -> 70.2 us  [shards(): pl.pallas_call(functools.partial(kernel, ny, nz, block), out_shape=jax.Sh...]
where the time goes in v2:
time: 71.7 us; the launch traced here: 71.5 us
  Pallas kernels  70.2 us (98%)
  local copies, waits for them, and re-layouts  1.33 us (2%)
    pallas_call x1, Pallas kernels, shards(): pl.pallas_call(functools.partial(kernel, ny, nz, block), out_shape=jax.Sh...  70.2 us

profile of v2, /device:TPU:1, one launch (start us, length us, event | category | flops | bytes accessed | tf_op | source)
XLA Modules:
  0.0 71.5 jit_solution(2815571928056066852)
XLA Ops:
  0.0 70.2 %layer.1 = bf16[2,4,1024]{2,1,0:T(4,128)(2,1)} custom-call(s32[2,2]{1,0:T(2,128)} %adapter_ref.1, s32[2,2]{1,0:T(2,128)} %live_ref.1, s32[64]{0:T(128)} %slot_ref.1, bf16[512,1024]{1,0:T(8,128)(2,1)} %bitcast.7, bf16[2,448,1024]{2,1,0:T(8,128)(2,1)} %bitcast.6, bf16[2,64,1024]{2,1,0:T(8,128)(2,1)} %bitcast.9, bf16[2,8,28672]{2,1,0:T(8,128)(2,1)} %bitcast.8, ...), custom_call_target="tpu_custom_call" | custom-call | tf_op jit(solution)/shard_map/layer/pallas_call | solution.py:403
  70.2 1.3 %copy.10 = bf16[2,4,1024]{2,1,0:T(4,128)(2,1)} copy(bf16[2,4,1024]{2,1,0:T(4,128)(2,1)} %layer.1) | data formatting | bytes 32768

commit v3 on v2

--- a/solution.py
+++ b/solution.py
@@ -57,10 +57,11 @@
     ny, nz, block,
     adapter_ref, live_ref, slot_ref, tok_h, w_h, s_h, e_h, d_h, out_ref,
     tok, w, sh, ev, dn,
-    sp, srx, sy, sz, pb, brx,
-    e1y, e1z, sel0, sel1, e2y, e2z, ets, erx, ecat,
-    hid, o0, o1, r0, r1, acc0, acc1, q0, q1, u0, u1,
-    ssem, rsem, lsem, os0, or0, os1, or1,
+    sp, srx, sy, sz, pb, brx, bsum,
+    e1y, e1z, sel0, sel1, e2y0, e2y1, e2z0, e2z1, ets, erx, ecat, hid,
+    fy, by, my, ay, hy, dy, accy, qy, uy,
+    fz, bz, mz, az, hz, dz, accz, qz, uz,
+    ssem, rsem, lsem, ysend, yrecv, zsend, zrecv,
 ):
     nt_ = lax.axis_size("tensor")
     p = lax.axis_index("pool")
@@ -137,9 +138,9 @@
     x_e1y, x_e1z = on_y(0), on_z(1)
     x_s, x_sy, x_sz = on_t(2), on_y(3), on_z(4)
     x_b = [on_t(5), on_t(6)]
-    x_e2y, x_e2z, x_et = on_z(7), on_y(8), on_t(9)
-    x_h = on_t(10)
-    x_q0, x_q1 = on_z(11), on_y(12)
+    x_e2y, x_e2z = [on_z(7), on_z(8)], [on_y(9), on_y(10)]
+    x_et, x_h = on_t(11), on_t(12)
+    x_qy, x_qz = [on_z(13), on_z(14)], [on_y(15), on_y(16)]
 
     for c in ecopies:
         c.wait()
@@ -189,59 +190,90 @@
     my_yo = lax.shift_right_logical(my_slot, zshift)
     my_zo = lax.bitwise_and(my_slot, nz - 1)
 
+    e2y, e2z = (e2y0, e2y1), (e2z0, e2z1)
     loads[5].wait()
     x_e1y.wait_recv()
-    for i in range(NSB):
-        sel0[i] = e1y[yo[i]]
-    x_e2y.start(lambda i: sel0.at[:, :, pl.ds(win(i), WIN)], lambda m: e2y.at[m])
+    for step in range(STEPS):
+        part = pl.ds(step * NBLK, NBLK)
+        for i in range(step * NBLK, (step + 1) * NBLK):
+            sel0[i] = e1y[yo[i]]
+        x_e2y[step].start(
+            lambda i, part=part: sel0.at[part, :, pl.ds(win(i), WIN)],
+            lambda m, step=step: e2y[step].at[m],
+        )
     own_z.wait()
     x_e1z.wait_recv()
-    for i in range(NSB):
-        sel1[i] = e1z[zo[i]]
-    x_e2z.start(lambda i: sel1.at[:, i], lambda m: e2z.at[m])
+    for step in range(STEPS):
+        part = pl.ds(step * NBLK, NBLK)
+        for i in range(step * NBLK, (step + 1) * NBLK):
+            sel1[i] = e1z[zo[i]]
+        x_e2z[step].start(
+            lambda i, part=part: sel1.at[part, i],
+            lambda m, step=step: e2z[step].at[m],
+        )
     x_sy.wait_recv()
     sz[z] = sy[my_yo]
     x_sz.start(lambda i: sz.at[z], lambda m: sz.at[m])
-    e2y[z] = sel0[:, :, pl.ds(win(z), WIN)]
-    e2z[y] = sel1[:, y]
-
-    sums = []
+    for step in range(STEPS):
+        part = pl.ds(step * NBLK, NBLK)
+        e2y[step][z] = sel0[part, :, pl.ds(win(z), WIN)]
+        e2z[step][y] = sel1[part, y]
+
     for k in range(2):
         x_b[k].wait_recv()
         total = pb[k, t].astype(F32)
         for i in tpeers:
             total = total + brx[k, i].astype(F32)
-        sums.append(total)
-
-    x_e2y.wait_recv()
-    for i in range(NSB):
-        ets[i, 0] = e2y[zo[i], i]
-    x_e2z.wait_recv()
-    for i in range(NSB):
-        ets[i, 1] = e2z[yo[i], i]
-    x_et.start(lambda i: ets.at[lax.div(i * rows_t, block)], lambda m: erx.at[m])
-    erx[t] = ets[mine]
-    x_sz.wait_recv()
-    shrunk = sz[my_zo]
-    x_et.wait_recv()
+        bsum[k] = total
+
+    x_et.src = lambda i: ets.at[lax.div(i * rows_t, block)]
+    x_et.dst = lambda m: erx.at[m]
+    x_h.src, x_h.dst = (lambda i: hid.at[t]), (lambda m: hid.at[m])
+    t_half = nt_ // STEPS
+    my_step = lax.div(t, t_half)
     rank_t = ranks // nt_
-    for k in range(2):
-        for i in range(nt_):
-            ecat[pl.ds(k * ranks + i * rank_t, rank_t)] = erx[i, k].astype(F32)
-    second = ecat[...]
-    rolled = pltpu.roll(second, WIN - 64, axis=1)
-    odd = lax.rem(z, 2) == 1
-    second = jnp.where(odd, rolled, second).astype(BF16)
-    lane = lax.broadcasted_iota(jnp.int32, shrunk.shape, 1)
-    zero = jnp.zeros_like(shrunk)
-    gate = jnp.dot(jnp.where(lane < ranks, shrunk, zero), second, preferred_element_type=F32)
-    up = jnp.dot(jnp.where(lane < ranks, zero, shrunk), second, preferred_element_type=F32)
-    gate = sums[0] + gate[:, :units]
-    up = sums[1] + up[:, :units]
-    hid[t] = (gate / (1.0 + jnp.exp(-gate)) * up).astype(BF16)
-    x_h.start(lambda i: hid.at[t], lambda m: hid.at[m])
+
+    def hidden_rows():
+        erx[t] = ets[mine]
+        x_sz.wait_recv()
+        shrunk = sz[my_zo]
+        x_et.wait_recv()
+        for k in range(2):
+            for i in range(nt_):
+                ecat[pl.ds(k * ranks + i * rank_t, rank_t)] = erx[i, k].astype(F32)
+        second = ecat[...]
+        rolled = pltpu.roll(second, WIN - 64, axis=1)
+        odd = lax.rem(z, 2) == 1
+        second = jnp.where(odd, rolled, second).astype(BF16)
+        lane = lax.broadcasted_iota(jnp.int32, shrunk.shape, 1)
+        zero = jnp.zeros_like(shrunk)
+        gate = jnp.dot(
+            jnp.where(lane < ranks, shrunk, zero), second, preferred_element_type=F32
+        )
+        up = jnp.dot(
+            jnp.where(lane < ranks, zero, shrunk), second, preferred_element_type=F32
+        )
+        gate = bsum[0] + gate[:, :units]
+        up = bsum[1] + up[:, :units]
+        hid[t] = (gate / (1.0 + jnp.exp(-gate)) * up).astype(BF16)
+        x_h.start(x_h.src, x_h.dst)
+
+    for step in range(STEPS):
+        x_e2y[step].wait_recv()
+        for i in range(NBLK):
+            ets[step * NBLK + i, 0] = e2y[step][zo[step * NBLK + i], i]
+        x_e2z[step].wait_recv()
+        for i in range(NBLK):
+            ets[step * NBLK + i, 1] = e2z[step][yo[step * NBLK + i], i]
+        for peer in tpeers:
+
+            @pl.when(lax.div(peer, t_half) == step)
+            def _(peer=peer):
+                x_et.copy(peer, x_et.src, x_et.dst, t).start()
+
+        pl.when(my_step == step)(hidden_rows)
+
     loads[4].wait()
-
     gps = nx // STEPS
     ypg = ny // gps
     rows_g = CORES * rows_t
@@ -256,93 +288,173 @@
     zz = lax.shift_right_logical(ri, gbits + ybits)
     perm = jnp.where(ci == yy * part_y + zz * grp + low, 1.0, 0.0).astype(BF16)
 
-    def copy_y(peer, source, step):
-        return pltpu.make_async_remote_copy(
-            src_ref=o0.at[peer, step],
-            dst_ref=r0.at[source, step],
-            send_sem=os0.at[peer, step],
-            recv_sem=or0.at[source, step],
-            device_id=ydev(peer),
-            device_id_type=MESH,
-        )
-
-    def copy_z(peer, source, chip):
-        return pltpu.make_async_remote_copy(
-            src_ref=o1.at[peer, chip],
-            dst_ref=r1.at[source, chip],
-            send_sem=os1.at[peer, chip],
-            recv_sem=or1.at[source, chip],
-            device_id=zdev(peer),
-            device_id_type=MESH,
-        )
-
-    for j, chip in enumerate(chips):
-        for i in tpeers[:1] if j == 0 else tpeers[CORES * j - 1:CORES * j + 1]:
-            x_h.wait_from(i)
+    def project(chip, step):
+        for i in range(CORES):
+            source = CORES * chip + i
+
+            @pl.when(source != t)
+            def _(source=source):
+                x_h.wait_from(source)
+
         h = hid[pl.ds(CORES * chip, CORES)].reshape(rows_g, units)
-        step = lax.div(chip, gps)
-        first = lax.rem(chip, gps) * ypg
-        part = jnp.dot(h, dn[:, :hw], preferred_element_type=F32).astype(BF16)
+        group = lax.rem(chip, gps)
+        first = group * ypg
+        part = jnp.dot(h, dn[:, :hw], preferred_element_type=F32)
         for i in range(ypg):
-            o0[first + i, step] = part[i * part_y:(i + 1) * part_y]
-        for i in range(ypg):
-            peer = first + lax.rem(y + i, ypg)
-
-            @pl.when(peer != y)
-            def _(peer=peer, step=step):
-                copy_y(peer, y, step).start()
-
+            piece = part[i * part_y:(i + 1) * part_y]
+            fy[step, first + i] = piece
+            by[step, first + i] = piece.astype(BF16)
         h = jnp.dot(perm, h, preferred_element_type=F32).astype(BF16)
-        part = jnp.dot(h, dn[:, hw:], preferred_element_type=F32).astype(BF16)
+        part = jnp.dot(h, dn[:, hw:], preferred_element_type=F32)
+        place = pl.ds(pl.multiple_of(group * part_z, part_z), part_z)
         for i in range(nz):
-            o1[i, chip] = part[i * part_z:(i + 1) * part_z]
-        for peer in zpeers:
-            copy_z(peer, z, chip).start()
-
-    total = o0[y].astype(F32)
-    for i in ypeers:
-        for step in range(STEPS):
-            copy_y(i, i, step).wait_recv()
-        total = total + r0[i].astype(F32)
-    acc0[...] = total
-    for i in range(nz):
-        q0[i] = acc0[:, pl.ds(i * grp, grp), :]
-    x_q0.start(lambda i: q0.at[i], lambda m: u0.at[m])
-
-    total = o1[z].astype(F32)
-    for i in zpeers:
-        for chip in range(nx):
-            copy_z(i, i, chip).wait_recv()
-        total = total + r1[i].astype(F32)
-    acc1[...] = total.reshape(STEPS, ny * grp, hw)
-    for i in range(ny):
-        q1[i] = acc1[:, pl.ds(i * grp, grp), :]
-    x_q1.start(lambda i: q1.at[i], lambda m: u1.at[m])
+            piece = part[i * part_z:(i + 1) * part_z]
+            fz[step, i, place] = piece
+            bz[step, i, place] = piece.astype(BF16)
+
+    class Ring:
+        def __init__(self, n, me, dev, full, short, merged, far, half, near, send, recv):
+            self.n, self.me, self.dev, self.full = n, me, dev, full
+            self.short, self.merged, self.far = short, merged, far
+            self.half, self.near, self.send, self.recv = half, near, send, recv
+            self.first = {1: (), 2: (4,), 8: (0, 1, 2, 3, 4, 5)}[n]
+            self.second = {1: (), 2: (), 8: (6, 7)}[n]
+
+        def at(self, offset):
+            return lax.rem(self.me + offset + self.n, self.n)
+
+        def copy(self, step, kind):
+            hh = hw // 2
+            hop, src, dst = {
+                0: (1, lambda: self.short.at[step, self.at(3)], self.far.at[step, 0]),
+                1: (-1, lambda: self.short.at[step, self.at(-3)], self.far.at[step, 1]),
+                2: (2, lambda: self.short.at[step, self.at(4), :, pl.ds(0, hh)],
+                    self.half.at[step, 0]),
+                3: (-2, lambda: self.short.at[step, self.at(4), :, pl.ds(hh, hh)],
+                    self.half.at[step, 1]),
+                4: (1, lambda: self.short.at[step, self.at(1)], self.near.at[step, 0]),
+                5: (-1, lambda: self.short.at[step, self.at(-1)], self.near.at[step, 1]),
+                6: (2, lambda: self.merged.at[step, 0], self.near.at[step, 2]),
+                7: (-2, lambda: self.merged.at[step, 1], self.near.at[step, 3]),
+            }[kind]
+            return pltpu.make_async_remote_copy(
+                src_ref=src(),
+                dst_ref=dst,
+                send_sem=self.send.at[step, kind],
+                recv_sem=self.recv.at[step, kind],
+                device_id=self.dev(self.at(hop)),
+                device_id_type=MESH,
+            )
+
+        def start(self, step):
+            for kind in self.first:
+                self.copy(step, kind).start()
+
+        def merge(self, step):
+            hh = hw // 2
+            for side in range(len(self.second)):
+                self.copy(step, side).wait_recv()
+                self.copy(step, 2 + side).wait_recv()
+                total = self.full[step, self.at((2, -2)[side])]
+                total = total + self.far[step, side].astype(F32)
+                more = self.half[step, side].astype(F32)
+                left, right = total[:, :hh], total[:, hh:]
+                if side == 0:
+                    left = left + more
+                else:
+                    right = right + more
+                self.merged[step, side, :, pl.ds(0, hh)] = left.astype(BF16)
+                self.merged[step, side, :, pl.ds(hh, hh)] = right.astype(BF16)
+                self.copy(step, 6 + side).start()
+
+        def total(self, step):
+            total = self.full[step, self.me]
+            for kind in self.first[4:] + self.second if self.n == 8 else self.first:
+                self.copy(step, kind).wait_recv()
+                total = total + self.near[step, kind - 4].astype(F32)
+            return total
+
+        def wait_send(self):
+            for step in range(STEPS):
+                for kind in self.first + self.second:
+                    self.copy(step, kind).wait_send()
+
+    ring_y = Ring(ny, y, ydev, fy, by, my, ay, hy, dy, ysend, yrecv)
+    ring_z = Ring(nz, z, zdev, fz, bz, mz, az, hz, dz, zsend, zrecv)
+    late = x >= gps
+    if gps == 2:
+        order = [
+            (jnp.where(late, nx - 1 - x, x), jnp.where(late, x - gps, 1 - x)),
+            (jnp.where(late, x, nx - 1 - x), jnp.where(late, 5 - x, x + gps)),
+        ]
+    else:
+        order = [(0,), (1,)]
+
+    def finish(step):
+        accy[...] = ring_y.total(step)
+        for i in range(nz):
+            qy[step, i] = accy[pl.ds(i * grp, grp), :]
+        x_qy[step].start(
+            lambda i: qy.at[step, i], lambda m: uy.at[step, m]
+        )
+        accz[...] = ring_z.total(step)
+        for i in range(ny):
+            qz[step, i] = accz[pl.ds(i * grp, grp), :]
+        x_qz[step].start(
+            lambda i: qz.at[step, i], lambda m: uz.at[step, m]
+        )
+
+    for chip in order[0]:
+        project(chip, 0)
+    ring_y.start(0)
+    ring_z.start(0)
+    project(order[1][0], 1)
+    ring_y.merge(0)
+    ring_z.merge(0)
+    for chip in order[1][1:]:
+        project(chip, 1)
+    ring_y.start(1)
+    ring_z.start(1)
+    finish(0)
+    ring_y.merge(1)
+    ring_z.merge(1)
+    finish(1)
 
     first = p * grp
     place = lax.rem(first, block) + lax.broadcasted_iota(jnp.int32, (grp, hw), 0)
     owner = lax.div(first, block)
-    for half, (xq, q, u, peers, me) in enumerate(
-        ((x_q0, q0, u0, zpeers, z), (x_q1, q1, u1, ypeers, y))
-    ):
-        total = q[me]
-        for i in peers:
-            xq.wait_from(i)
-            total = total + u[i]
-        for step in range(STEPS):
-            keep = place < live_ref[step, owner]
+    for step in range(STEPS):
+        keep = place < live_ref[step, owner]
+        for half, (xq, q, u, peers, me) in enumerate(
+            ((x_qy, qy, uy, zpeers, z), (x_qz, qz, uz, ypeers, y))
+        ):
+            total = q[step, me]
+            for i in peers:
+                xq[step].wait_from(i)
+                total = total + u[step, i]
             out_ref[step, :, half * hw:(half + 1) * hw] = jnp.where(
-                keep, total[step], 0.0
+                keep, total, 0.0
             ).astype(BF16)
 
-    for e in (x_e1y, x_e1z, x_s, *x_b, x_sy, x_sz, x_e2y, x_e2z, x_et, x_h, x_q0, x_q1):
+    for e in (x_e1y, x_e1z, x_s, *x_b, x_sy, x_sz, *x_e2y, *x_e2z, x_et, x_h,
+              *x_qy, *x_qz, ring_y, ring_z):
         e.wait_send()
-    for i in ypeers:
-        for step in range(STEPS):
-            copy_y(i, y, step).wait_send()
-    for i in zpeers:
-        for chip in range(nx):
-            copy_z(i, z, chip).wait_send()
+
+
+def ring_scratch(n, other, grp, hw):
+    rows = other * grp
+    vmem = pltpu.VMEM
+    return [
+        vmem((STEPS, n, rows, hw), F32),
+        vmem((STEPS, n, rows, hw), BF16),
+        vmem((STEPS, 2, rows, hw), BF16),
+        vmem((STEPS, 2, rows, hw), BF16),
+        vmem((STEPS, 2, rows, hw // 2), BF16),
+        vmem((STEPS, 4, rows, hw), BF16),
+        vmem((rows, hw), F32),
+        vmem((STEPS, other, grp, hw), F32),
+        vmem((STEPS, other, grp, hw), F32),
+    ]
 
 
 def shards(ny, nz, block, tokens, gate_up, down, shrink, expand, adapter, live, slots):
@@ -355,8 +467,6 @@
     grp = rows // (ny * nz)
     span = nz * units
     hw = width // 2
-    nx = n_t // CORES
-    part_z = ny // (nx // steps) * grp
     any_spec = pl.BlockSpec(memory_space=pl.ANY)
     smem = pl.BlockSpec(memory_space=pltpu.SMEM)
     vmem = pltpu.VMEM
@@ -372,33 +482,28 @@
         vmem((nz, rows_t, 2 * ranks), BF16),
         vmem((2, n_t, rows_t, units), BF16),
         vmem((2, n_t, rows_t, units), BF16),
+        vmem((2, rows_t, units), F32),
         vmem((ny, rank_t, span), BF16),
         vmem((nz, ny, rank_t, WIN), BF16),
         vmem((NSB, rank_t, span), BF16),
         vmem((NSB, ny, rank_t, WIN), BF16),
-        vmem((nz, NSB, rank_t, WIN), BF16),
-        vmem((ny, NSB, rank_t, WIN), BF16),
+        vmem((nz, NBLK, rank_t, WIN), BF16),
+        vmem((nz, NBLK, rank_t, WIN), BF16),
+        vmem((ny, NBLK, rank_t, WIN), BF16),
+        vmem((ny, NBLK, rank_t, WIN), BF16),
         vmem((NSB, 2, rank_t, WIN), BF16),
         vmem((n_t, 2, rank_t, WIN), BF16),
         vmem((2 * ranks, WIN), F32),
         vmem((n_t, rows_t, units), BF16),
-        vmem((ny, steps, nz * grp, hw), BF16),
-        vmem((nz, nx, part_z, hw), BF16),
-        vmem((ny, steps, nz * grp, hw), BF16),
-        vmem((nz, nx, part_z, hw), BF16),
-        vmem((steps, nz * grp, hw), F32),
-        vmem((steps, ny * grp, hw), F32),
-        vmem((nz, steps, grp, hw), F32),
-        vmem((ny, steps, grp, hw), F32),
-        vmem((nz, steps, grp, hw), F32),
-        vmem((ny, steps, grp, hw), F32),
-        pltpu.SemaphoreType.DMA((13, max(ny, nz, n_t))),
-        pltpu.SemaphoreType.DMA((13, max(ny, nz, n_t))),
+        *ring_scratch(ny, nz, grp, hw),
+        *ring_scratch(nz, ny, grp, hw),
+        pltpu.SemaphoreType.DMA((17, max(ny, nz, n_t))),
+        pltpu.SemaphoreType.DMA((17, max(ny, nz, n_t))),
         pltpu.SemaphoreType.DMA((7 + ny,)),
-        pltpu.SemaphoreType.DMA((ny, steps)),
-        pltpu.SemaphoreType.DMA((ny, steps)),
-        pltpu.SemaphoreType.DMA((nz, nx)),
-        pltpu.SemaphoreType.DMA((nz, nx)),
+        pltpu.SemaphoreType.DMA((steps, 8)),
+        pltpu.SemaphoreType.DMA((steps, 8)),
+        pltpu.SemaphoreType.DMA((steps, 8)),
+        pltpu.SemaphoreType.DMA((steps, 8)),
     ]
     return pl.pallas_call(
         functools.partial(kernel, ny, nz, block),

time: 71.7 us -> 78.9 us (1.10)
  Pallas kernels: 70.2 us -> 77.3 us
    pallas_call x1, Pallas kernels: 70.2 us -> 77.3 us  [shards(): pl.pallas_call(functools.partial(kernel, ny, nz, block), out_shape=jax.Sh...]
where the time goes in v3:
time: 78.9 us; the launch traced here: 78.7 us
  Pallas kernels  77.3 us (98%)
  local copies, waits for them, and re-layouts  1.33 us (2%)
    pallas_call x1, Pallas kernels, shards(): pl.pallas_call(functools.partial(kernel, ny, nz, block), out_shape=jax.Sh...  77.3 us

profile of v3, /device:TPU:1, one launch (start us, length us, event | category | flops | bytes accessed | tf_op | source)
XLA Modules:
  0.0 78.7 jit_solution(12897856177328478323)
XLA Ops:
  0.0 77.3 %layer.1 = bf16[2,4,1024]{2,1,0:T(4,128)(2,1)} custom-call(s32[2,2]{1,0:T(2,128)} %adapter_ref.1, s32[2,2]{1,0:T(2,128)} %live_ref.1, s32[64]{0:T(128)} %slot_ref.1, bf16[512,1024]{1,0:T(8,128)(2,1)} %bitcast.7, bf16[2,448,1024]{2,1,0:T(8,128)(2,1)} %bitcast.6, bf16[2,64,1024]{2,1,0:T(8,128)(2,1)} %bitcast.9, bf16[2,8,28672]{2,1,0:T(8,128)(2,1)} %bitcast.8, ...), custom_call_target="tpu_custom_call" | custom-call | tf_op jit(solution)/shard_map/layer/pallas_call | solution.py:508
  77.3 1.3 %copy.10 = bf16[2,4,1024]{2,1,0:T(4,128)(2,1)} copy(bf16[2,4,1024]{2,1,0:T(4,128)(2,1)} %layer.1) | data formatting | bytes 32768

commit v4 on v3

--- a/solution.py
+++ b/solution.py
@@ -57,8 +57,8 @@
     ny, nz, block,
     adapter_ref, live_ref, slot_ref, tok_h, w_h, s_h, e_h, d_h, out_ref,
     tok, w, sh, ev, dn,
-    sp, srx, sy, sz, pb, brx, bsum,
-    e1y, e1z, sel0, sel1, e2y0, e2y1, e2z0, e2z1, ets, erx, ecat, hid,
+    sp, srx, sy, sz, pb0, brx0, pb1, brx1, bsum,
+    e1y, e1z, sel0, sel1, e2y, e2z, ets, erx, ecat, hid,
     fy, by, my, ay, hy, dy, accy, qy, uy,
     fz, bz, mz, az, hz, dz, accz, qz, uz,
     ssem, rsem, lsem, ysend, yrecv, zsend, zrecv,
@@ -138,8 +138,15 @@
     x_e1y, x_e1z = on_y(0), on_z(1)
     x_s, x_sy, x_sz = on_t(2), on_y(3), on_z(4)
     x_b = [on_t(5), on_t(6)]
-    x_e2y, x_e2z = [on_z(7), on_z(8)], [on_y(9), on_y(10)]
-    x_et, x_h = on_t(11), on_t(12)
+    x_e2y, x_e2z = on_z(7), on_y(8)
+    x_et, x_h = [on_t(11), on_t(17)], on_t(12)
+    if nx == 4:
+        pair = x + 1 - 2 * lax.rem(x, 2)
+        x_h.peers = [other] + [
+            CORES * c + lax.rem(core + i, CORES)
+            for c in (pair, lax.rem(x + 2, nx), nx - 1 - x)
+            for i in range(CORES)
+        ]
     x_qy, x_qz = [on_z(13), on_z(14)], [on_y(15), on_y(16)]
 
     for c in ecopies:
@@ -165,11 +172,13 @@
 
     loads[3].wait()
 
+    pb, brx = (pb0, pb1), (brx0, brx1)
+
     def base(k):
-        part = nt(tok[...], w[k]).astype(BF16)
+        part = nt(tok[...], w[k]).astype(pb[k].dtype)
         for i in range(nt_):
-            pb[k, i] = part[i * rows_t:(i + 1) * rows_t]
-        x_b[k].start(lambda i: pb.at[k, i], lambda m: brx.at[k, m])
+            pb[k][i] = part[i * rows_t:(i + 1) * rows_t]
+        x_b[k].start(lambda i: pb[k].at[i], lambda m: brx[k].at[m])
 
     base(0)
 
@@ -190,57 +199,43 @@
     my_yo = lax.shift_right_logical(my_slot, zshift)
     my_zo = lax.bitwise_and(my_slot, nz - 1)
 
-    e2y, e2z = (e2y0, e2y1), (e2z0, e2z1)
     loads[5].wait()
     x_e1y.wait_recv()
-    for step in range(STEPS):
-        part = pl.ds(step * NBLK, NBLK)
-        for i in range(step * NBLK, (step + 1) * NBLK):
-            sel0[i] = e1y[yo[i]]
-        x_e2y[step].start(
-            lambda i, part=part: sel0.at[part, :, pl.ds(win(i), WIN)],
-            lambda m, step=step: e2y[step].at[m],
-        )
+    for i in range(NSB):
+        sel0[i] = e1y[yo[i]]
+    x_e2y.start(lambda i: sel0.at[:, :, pl.ds(win(i), WIN)], lambda m: e2y.at[m])
     own_z.wait()
     x_e1z.wait_recv()
-    for step in range(STEPS):
-        part = pl.ds(step * NBLK, NBLK)
-        for i in range(step * NBLK, (step + 1) * NBLK):
-            sel1[i] = e1z[zo[i]]
-        x_e2z[step].start(
-            lambda i, part=part: sel1.at[part, i],
-            lambda m, step=step: e2z[step].at[m],
-        )
+    for i in range(NSB):
+        sel1[i] = e1z[zo[i]]
+    x_e2z.start(lambda i: sel1.at[:, i], lambda m: e2z.at[m])
     x_sy.wait_recv()
     sz[z] = sy[my_yo]
     x_sz.start(lambda i: sz.at[z], lambda m: sz.at[m])
-    for step in range(STEPS):
-        part = pl.ds(step * NBLK, NBLK)
-        e2y[step][z] = sel0[part, :, pl.ds(win(z), WIN)]
-        e2z[step][y] = sel1[part, y]
+    e2y[z] = sel0[:, :, pl.ds(win(z), WIN)]
+    e2z[y] = sel1[:, y]
 
     for k in range(2):
         x_b[k].wait_recv()
-        total = pb[k, t].astype(F32)
+        total = pb[k][t].astype(F32)
         for i in tpeers:
-            total = total + brx[k, i].astype(F32)
+            total = total + brx[k][i].astype(F32)
         bsum[k] = total
 
-    x_et.src = lambda i: ets.at[lax.div(i * rows_t, block)]
-    x_et.dst = lambda m: erx.at[m]
     x_h.src, x_h.dst = (lambda i: hid.at[t]), (lambda m: hid.at[m])
-    t_half = nt_ // STEPS
-    my_step = lax.div(t, t_half)
+    my_step = lax.div(t, nt_ // STEPS)
     rank_t = ranks // nt_
 
     def hidden_rows():
-        erx[t] = ets[mine]
+        for k in range(2):
+            erx[k, t] = ets[k, mine]
         x_sz.wait_recv()
         shrunk = sz[my_zo]
-        x_et.wait_recv()
+        for k in range(2):
+            x_et[k].wait_recv()
         for k in range(2):
             for i in range(nt_):
-                ecat[pl.ds(k * ranks + i * rank_t, rank_t)] = erx[i, k].astype(F32)
+                ecat[pl.ds(k * ranks + i * rank_t, rank_t)] = erx[k, i].astype(F32)
         second = ecat[...]
         rolled = pltpu.roll(second, WIN - 64, axis=1)
         odd = lax.rem(z, 2) == 1
@@ -258,20 +253,15 @@
         hid[t] = (gate / (1.0 + jnp.exp(-gate)) * up).astype(BF16)
         x_h.start(x_h.src, x_h.dst)
 
-    for step in range(STEPS):
-        x_e2y[step].wait_recv()
-        for i in range(NBLK):
-            ets[step * NBLK + i, 0] = e2y[step][zo[step * NBLK + i], i]
-        x_e2z[step].wait_recv()
-        for i in range(NBLK):
-            ets[step * NBLK + i, 1] = e2z[step][yo[step * NBLK + i], i]
-        for peer in tpeers:
-
-            @pl.when(lax.div(peer, t_half) == step)
-            def _(peer=peer):
-                x_et.copy(peer, x_et.src, x_et.dst, t).start()
-
-        pl.when(my_step == step)(hidden_rows)
+    for k, (e, ref, own) in enumerate(((x_e2y, e2y, zo), (x_e2z, e2z, yo))):
+        e.wait_recv()
+        for i in range(NSB):
+            ets[k, i] = ref[own[i], i]
+        x_et[k].start(
+            lambda i, k=k: ets.at[k, lax.div(i * rows_t, block)],
+            lambda m, k=k: erx.at[k, m],
+        )
+    hidden_rows()
 
     loads[4].wait()
     gps = nx // STEPS
@@ -381,14 +371,9 @@
 
     ring_y = Ring(ny, y, ydev, fy, by, my, ay, hy, dy, ysend, yrecv)
     ring_z = Ring(nz, z, zdev, fz, bz, mz, az, hz, dz, zsend, zrecv)
-    late = x >= gps
-    if gps == 2:
-        order = [
-            (jnp.where(late, nx - 1 - x, x), jnp.where(late, x - gps, 1 - x)),
-            (jnp.where(late, x, nx - 1 - x), jnp.where(late, 5 - x, x + gps)),
-        ]
-    else:
-        order = [(0,), (1,)]
+    order = [(x,), (1 - x,)] if gps == 1 else [
+        (x, x + 1 - 2 * lax.rem(x, 2)), (nx - 1 - x, lax.rem(x + gps, nx))
+    ]
 
     def finish(step):
         accy[...] = ring_y.total(step)
@@ -404,39 +389,35 @@
             lambda i: qz.at[step, i], lambda m: uz.at[step, m]
         )
 
-    for chip in order[0]:
-        project(chip, 0)
-    ring_y.start(0)
-    ring_z.start(0)
-    project(order[1][0], 1)
-    ring_y.merge(0)
-    ring_z.merge(0)
-    for chip in order[1][1:]:
-        project(chip, 1)
-    ring_y.start(1)
-    ring_z.start(1)
-    finish(0)
-    ring_y.merge(1)
-    ring_z.merge(1)
-    finish(1)
+    for turn in range(STEPS):
+        for chip in order[turn]:
+            project(chip, turn)
+        ring_y.start(turn)
+        ring_z.start(turn)
+    for turn in range(STEPS):
+        ring_y.merge(turn)
+        ring_z.merge(turn)
+    for turn in range(STEPS):
+        finish(turn)
 
     first = p * grp
     place = lax.rem(first, block) + lax.broadcasted_iota(jnp.int32, (grp, hw), 0)
     owner = lax.div(first, block)
-    for step in range(STEPS):
+    for turn in range(STEPS):
+        step = lax.rem(my_step + turn, STEPS)
         keep = place < live_ref[step, owner]
         for half, (xq, q, u, peers, me) in enumerate(
             ((x_qy, qy, uy, zpeers, z), (x_qz, qz, uz, ypeers, y))
         ):
-            total = q[step, me]
+            total = q[turn, me]
             for i in peers:
-                xq[step].wait_from(i)
-                total = total + u[step, i]
+                xq[turn].wait_from(i)
+                total = total + u[turn, i]
             out_ref[step, :, half * hw:(half + 1) * hw] = jnp.where(
                 keep, total, 0.0
             ).astype(BF16)
 
-    for e in (x_e1y, x_e1z, x_s, *x_b, x_sy, x_sz, *x_e2y, *x_e2z, x_et, x_h,
+    for e in (x_e1y, x_e1z, x_s, *x_b, x_sy, x_sz, x_e2y, x_e2z, *x_et, x_h,
               *x_qy, *x_qz, ring_y, ring_z):
         e.wait_send()
 
@@ -480,25 +461,25 @@
         vmem((n_t, rows_t, 2 * ranks), F32),
         vmem((ny, rows_t, 2 * ranks), BF16),
         vmem((nz, rows_t, 2 * ranks), BF16),
-        vmem((2, n_t, rows_t, units), BF16),
-        vmem((2, n_t, rows_t, units), BF16),
+        vmem((n_t, rows_t, units), F32),
+        vmem((n_t, rows_t, units), F32),
+        vmem((n_t, rows_t, units), BF16),
+        vmem((n_t, rows_t, units), BF16),
         vmem((2, rows_t, units), F32),
         vmem((ny, rank_t, span), BF16),
         vmem((nz, ny, rank_t, WIN), BF16),
         vmem((NSB, rank_t, span), BF16),
         vmem((NSB, ny, rank_t, WIN), BF16),
-        vmem((nz, NBLK, rank_t, WIN), BF16),
-        vmem((nz, NBLK, rank_t, WIN), BF16),
-        vmem((ny, NBLK, rank_t, WIN), BF16),
-        vmem((ny, NBLK, rank_t, WIN), BF16),
-        vmem((NSB, 2, rank_t, WIN), BF16),
-        vmem((n_t, 2, rank_t, WIN), BF16),
+        vmem((nz, NSB, rank_t, WIN), BF16),
+        vmem((ny, NSB, rank_t, WIN), BF16),
+        vmem((2, NSB, rank_t, WIN), BF16),
+        vmem((2, n_t, rank_t, WIN), BF16),
         vmem((2 * ranks, WIN), F32),
         vmem((n_t, rows_t, units), BF16),
         *ring_scratch(ny, nz, grp, hw),
         *ring_scratch(nz, ny, grp, hw),
-        pltpu.SemaphoreType.DMA((17, max(ny, nz, n_t))),
-        pltpu.SemaphoreType.DMA((17, max(ny, nz, n_t))),
+        pltpu.SemaphoreType.DMA((18, max(ny, nz, n_t))),
+        pltpu.SemaphoreType.DMA((18, max(ny, nz, n_t))),
         pltpu.SemaphoreType.DMA((7 + ny,)),
         pltpu.SemaphoreType.DMA((steps, 8)),
         pltpu.SemaphoreType.DMA((steps, 8)),

time: 78.9 us -> 70.7 us (0.90)
  Pallas kernels: 77.3 us -> 68.6 us
    pallas_call x1, Pallas kernels: 77.3 us -> 68.6 us  [shards(): pl.pallas_call(functools.partial(kernel, ny, nz, block), out_shape=jax.Sh...]
where the time goes in v4:
time: 70.7 us; the launch traced here: 70 us
  Pallas kernels  68.6 us (97%)
  local copies, waits for them, and re-layouts  1.33 us (2%)
    pallas_call x1, Pallas kernels, shards(): pl.pallas_call(functools.partial(kernel, ny, nz, block), out_shape=jax.Sh...  68.6 us

profile of v4, /device:TPU:1, one launch (start us, length us, event | category | flops | bytes accessed | tf_op | source)
XLA Modules:
  0.0 70.0 jit_solution(9738870220639253098)
XLA Ops:
  0.0 68.6 %layer.1 = bf16[2,4,1024]{2,1,0:T(4,128)(2,1)} custom-call(s32[2,2]{1,0:T(2,128)} %adapter_ref.1, s32[2,2]{1,0:T(2,128)} %live_ref.1, s32[64]{0:T(128)} %slot_ref.1, bf16[512,1024]{1,0:T(8,128)(2,1)} %bitcast.7, bf16[2,448,1024]{2,1,0:T(8,128)(2,1)} %bitcast.6, bf16[2,64,1024]{2,1,0:T(8,128)(2,1)} %bitcast.9, bf16[2,8,28672]{2,1,0:T(8,128)(2,1)} %bitcast.8, ...), custom_call_target="tpu_custom_call" | custom-call | tf_op jit(solution)/shard_map/layer/pallas_call | solution.py:489
  68.7 1.3 %copy.10 = bf16[2,4,1024]{2,1,0:T(4,128)(2,1)} copy(bf16[2,4,1024]{2,1,0:T(4,128)(2,1)} %layer.1) | data formatting | bytes 32768

commit v5 on v4

--- a/solution.py
+++ b/solution.py
@@ -83,8 +83,8 @@
     hw = width // 2
     hops = [0] + sorted(range(1, nx), key=lambda d: min(d, nx - d))
     chips = [lax.rem(x + d, nx) for d in hops]
-    ypeers = [lax.rem(y + k, ny) for k in range(1, ny)]
-    zpeers = [lax.rem(z + k, nz) for k in range(1, nz)]
+    ypeers = [lax.rem(y + k, ny) for k in sorted(range(1, ny), key=lambda k: -min(k, ny - k))]
+    zpeers = [lax.rem(z + k, nz) for k in sorted(range(1, nz), key=lambda k: -min(k, nz - k))]
     other = CORES * x + (CORES - 1 - core)
     tpeers = [other] + [
         CORES * c + lax.rem(core + i, CORES) for c in chips[1:] for i in range(CORES)

time: 70.7 us -> 68.8 us (0.973)
  Pallas kernels: 68.6 us -> 67 us
    pallas_call x1, Pallas kernels: 68.6 us -> 67 us  [shards(): pl.pallas_call(functools.partial(kernel, ny, nz, block), out_shape=jax.Sh...]
where the time goes in v5:
time: 68.8 us; the launch traced here: 68.3 us
  Pallas kernels  67 us (97%)
  local copies, waits for them, and re-layouts  1.33 us (2%)
    pallas_call x1, Pallas kernels, shards(): pl.pallas_call(functools.partial(kernel, ny, nz, block), out_shape=jax.Sh...  67 us

profile of v5, /device:TPU:1, one launch (start us, length us, event | category | flops | bytes accessed | tf_op | source)
XLA Modules:
  0.0 68.3 jit_solution(7878110881084144500)
XLA Ops:
  0.0 67.0 %layer.1 = bf16[2,4,1024]{2,1,0:T(4,128)(2,1)} custom-call(s32[2,2]{1,0:T(2,128)} %adapter_ref.1, s32[2,2]{1,0:T(2,128)} %live_ref.1, s32[64]{0:T(128)} %slot_ref.1, bf16[512,1024]{1,0:T(8,128)(2,1)} %bitcast.7, bf16[2,448,1024]{2,1,0:T(8,128)(2,1)} %bitcast.6, bf16[2,64,1024]{2,1,0:T(8,128)(2,1)} %bitcast.9, bf16[2,8,28672]{2,1,0:T(8,128)(2,1)} %bitcast.8, ...), custom_call_target="tpu_custom_call" | custom-call | tf_op jit(solution)/shard_map/layer/pallas_call | solution.py:489
  67.0 1.3 %copy.10 = bf16[2,4,1024]{2,1,0:T(4,128)(2,1)} copy(bf16[2,4,1024]{2,1,0:T(4,128)(2,1)} %layer.1) | data formatting | bytes 32768
